TPU v7x, 32 devices: a whole 2x2x4 slice. The times are simulated.
32 devices in a mesh: band: 4 (over y, x), ga: 8 (over z, core).
Axes of the slice: x: 2, y: 2, z: 4, core: 2. Of those that a mesh axis runs over, the one named last changes fastest.
Arguments:
- psi: float32 [4096, 4096], P('band', 'ga'), may hold values from -6 to 6
- lower: float32 [4096, 4096], P('band', 'ga'), as said below
Outputs:
- orthonormal: float32 [4096, 4096], P('band', 'ga')
- block_intersection: float32 [4096, 1024], P('band')
Inputs may be any that keep to these rules, and one draw needn't show every extreme that they name: lower is lower triangular with its diagonal between 1 and 2.
All inputs are finite; a program needn't handle non-finite values.
Results may differ from a plain program's by a relative error of at most 0.00022.
Values sent between devices are 32-bit elements; how exact they have to be, the bound alone decides.
A program may use at most 64 MiB of HBM per device.

v0:
```python
import jax
import jax.numpy as jnp
from jax import lax
from jax.sharding import PartitionSpec as P


def from_root(value, axis, source):
    kept = jnp.where(lax.axis_index(axis) == source, value, 0).astype(value.dtype)
    return lax.psum(kept, axis)


def local(psi, lower):
    myblock = lax.axis_index("band")
    sections = lax.axis_size("band")
    nrows = psi.shape[0]
    width = psi.shape[1]
    full_rows = lax.all_gather(lower, "ga", axis=1, tiled=True)
    own_tile = lax.dynamic_slice_in_dim(full_rows, myblock * nrows, nrows, 1)

    def finish(rhs):
        return jax.scipy.linalg.solve_triangular(own_tile, rhs, lower=True)

    def nothing(rhs):
        return jnp.zeros_like(rhs)

    pieces = 1
    span = width // pieces

    def section(section_idx, carry):
        totals, results = carry
        tile = lax.dynamic_slice_in_dim(full_rows, section_idx * nrows, nrows, 1)
        rhs = psi - totals[0]
        ready = lax.cond(myblock == section_idx, finish, nothing, rhs)
        arrived = from_root(ready, "band", section_idx)
        new_results = [jnp.where(myblock == section_idx, ready, results[0])]
        term = jnp.dot(
            tile, arrived, precision=lax.Precision.HIGHEST, preferred_element_type=jnp.float32
        )
        new_totals = [jnp.where(section_idx < myblock, totals[0] + term, totals[0])]
        return (tuple(new_totals), tuple(new_results))

    blank = tuple((jnp.zeros((nrows, span), jnp.float32) for piece in range(pieces)))
    totals, results = lax.fori_loop(0, sections, section, (blank, blank))
    solved = results[0]
    local_intersection = jnp.dot(
        solved, solved.T, precision=lax.Precision.HIGHEST, preferred_element_type=jnp.float32
    )
    intersection = lax.psum(local_intersection, "ga") / (width * lax.axis_size("ga"))
    return (solved, intersection)


def solution(mesh):
    return jax.shard_map(
        local,
        mesh=mesh,
        in_specs=(P("band", "ga"), P("band", "ga")),
        out_specs=(P("band", "ga"), P("band", None)),
        check_vma=False,
    )
```

profile of v0, /device:TPU:0, one launch (start us, length us, event | category | flops | bytes accessed | tf_op | source)
XLA Modules:
  0.0 1144.7 jit_solution(381688450208989229)
XLA Ops:
  7.9 155.5 %all-gather.2.cloned.1.call-done = f32[1024,4096]{1,0:T(8,128)} async-done(((f32[1024,512]{1,0:T(8,128)}), f32[1024,4096]{1,0:T(8,128)}) %all-gather.2.cloned.1.call-update) | async-done | bytes 16777232 | tf_op jit(solution)/shard_map/all_gather | solution.py:17
  163.4 4.8 constant_dynamic-slice_fusion.1
  168.2 857.6 %while.20 = (s32[]{:T(128)}, f32[1024,512]{1,0:T(8,128)}, f32[1024,512]{1,0:T(8,128)}, s32[]{:T(128)}, f32[1024,4096]{1,0:T(8,128)}, /*index=5*/f32[1024,1024]{1...) while((s32[]{:T(128)}, f32[1024,512]{1,0:T(8,128)}, ...), condition=%wide.region_4.5_spmd.clone, body=%wide.region_0.4_spmd.clone.sunk | while | flops 10074390528 | bytes 73794136 | solution.py:43
  168.4 129.2 %conditional.3 = (f32[1024,512]{1,0:T(8,128)}) conditional(s32[]{:T(128)} %convert_element_type.20, () %tuple.91, (f32[1024,1024]{1,0:T(8,128)}, f32[1024,512]{1,0:T(8,128)}, f32[1024,512]{1,0:T(8,128)S(1)}) %tuple.92), branch_computations={%region_1.0_spmd, %region_2.2_spmd} | conditional | flops 3628269568 | bytes 38142244 | solution.py:33
  168.5 4.7 fusion
  173.2 22.5 %while.19 = (s32[]{:T(128)}, f32[1024,1024]{1,0:T(8,128)}, s32[8,2]{0,1:T(2,128)S(1)}, f32[8,128,128]{2,1,0:T(8,128)S(1)}, s32[]{:T(128)}) while((s32[]{:T(128)}, f32[1024,1024]{1,0:T(8,128)}, s32[8,2]{0,1:T(2,128)S(1)}, f32[8,128,128]{2,1,0:T(8,128)S(1)}, s32[]{:T(128)}) %tuple.95), condition=%wide.while_cond, body=%wide.while_body.sunk | while | flops 2 | bytes 131181 | solution.py:21
  173.8 2.2 bitcast_dynamic-update-slice_fusion.2
  176.6 2.2 bitcast_dynamic-update-slice_fusion.2
  179.4 2.2 bitcast_dynamic-update-slice_fusion.2
  182.3 2.2 bitcast_dynamic-update-slice_fusion.2
  185.1 2.2 bitcast_dynamic-update-slice_fusion.2
  187.9 2.2 bitcast_dynamic-update-slice_fusion.2
  190.7 2.2 bitcast_dynamic-update-slice_fusion.2
  193.5 2.1 bitcast_dynamic-update-slice_fusion.2
  195.7 78.6 %custom-call.3 = f32[8,128,128]{1,2,0:T(8,128)S(1)} custom-call(f32[8,128,128]{2,1,0:T(8,128)S(1)} %get-tuple-element.206), custom_call_target="InvertDiagBlocksLowerTriangular" | custom-call | tf_op jit(solution)/shard_map/while/body/eval_jaxpr/cond/branch_1_fun/jit(_solve_triangular)/triangular_solve | solution.py:21
  274.3 2.1 sub.8
  294.3 2.2 convolution_subtract_fusion
  297.7 4.3 select_select_fusion.2
  302.0 66.0 %all-reduce.5.cloned.1.call-done = f32[1024,512]{1,0:T(8,128)} async-done(((f32[1024,512]{1,0:T(8,128)}), f32[1024,512]{1,0:T(8,128)}) %all-reduce.5.cloned.1.call-update) | async-done | bytes 2097168 | tf_op jit(solution)/shard_map/while/body/eval_jaxpr/psum | solution.py:9
  368.0 10.3 add_select_fusion.2
  381.7 4.9 select_select_fusion.2
  386.7 197.2 %all-reduce.5.cloned.1.call-done = f32[1024,512]{1,0:T(8,128)} async-done(((f32[1024,512]{1,0:T(8,128)}), f32[1024,512]{1,0:T(8,128)}) %all-reduce.5.cloned.1.call-update) | async-done | bytes 2097168 | tf_op jit(solution)/shard_map/while/body/eval_jaxpr/psum | solution.py:9
  583.9 10.3 add_select_fusion.2
  597.6 4.9 select_select_fusion.2
  602.6 197.1 %all-reduce.5.cloned.1.call-done = f32[1024,512]{1,0:T(8,128)} async-done(((f32[1024,512]{1,0:T(8,128)}), f32[1024,512]{1,0:T(8,128)}) %all-reduce.5.cloned.1.call-update) | async-done | bytes 2097168 | tf_op jit(solution)/shard_map/while/body/eval_jaxpr/psum | solution.py:9
  799.6 10.3 add_select_fusion.2
  813.4 4.9 select_select_fusion.2
  818.3 197.2 %all-reduce.5.cloned.1.call-done = f32[1024,512]{1,0:T(8,128)} async-done(((f32[1024,512]{1,0:T(8,128)}), f32[1024,512]{1,0:T(8,128)}) %all-reduce.5.cloned.1.call-update) | async-done | bytes 2097168 | tf_op jit(solution)/shard_map/while/body/eval_jaxpr/psum | solution.py:9
  1015.5 10.3 add_select_fusion.2
  1025.8 10.3 fusion.40
  1036.1 96.6 %all-reduce.3.cloned.1.call-done = f32[1024,1024]{1,0:T(8,128)} async-done(((f32[1024,1024]{1,0:T(8,128)}), f32[1024,1024]{1,0:T(8,128)}) %all-reduce.3.cloned.1.call-update) | async-done | bytes 4194320 | tf_op jit(solution)/shard_map/psum | solution.py:48
  1132.8 5.0 broadcast_multiply_fusion
  (57 shorter events, 40.1 us)
Async XLA Ops:
  7.2 156.3 %all-gather.2.cloned.1.call-start = ((), (), s32[]{:S(2)}) async-start(), calls=%async_computation | async-start | bytes 18874368 | tf_op jit(solution)/shard_map/all_gather | solution.py:17
  168.2 199.8 %all-reduce.5.cloned.1.call-start = ((), (), s32[]{:S(2)}) async-start(), calls=%async_computation.2 | async-start | bytes 4194304 | tf_op jit(solution)/shard_map/while/body/eval_jaxpr/psum | solution.py:9
  378.3 205.6 %all-reduce.5.cloned.1.call-start = ((), (), s32[]{:S(2)}) async-start(), calls=%async_computation.2 | async-start | bytes 4194304 | tf_op jit(solution)/shard_map/while/body/eval_jaxpr/psum | solution.py:9
  594.1 205.5 %all-reduce.5.cloned.1.call-start = ((), (), s32[]{:S(2)}) async-start(), calls=%async_computation.2 | async-start | bytes 4194304 | tf_op jit(solution)/shard_map/while/body/eval_jaxpr/psum | solution.py:9
  809.9 205.6 %all-reduce.5.cloned.1.call-start = ((), (), s32[]{:S(2)}) async-start(), calls=%async_computation.2 | async-start | bytes 4194304 | tf_op jit(solution)/shard_map/while/body/eval_jaxpr/psum | solution.py:9
  1025.8 107.0 %all-reduce.3.cloned.1.call-start = ((), (), s32[]{:S(2)}) async-start(), calls=%async_computation.1 | async-start | bytes 8388608 | tf_op jit(solution)/shard_map/psum | solution.py:48
Sparse Core Ops, SparseCore 0:
  9.6 153.7 all-gather.1
  302.1 65.8 all-reduce.4
  386.8 197.0 all-reduce.4
  602.7 196.9 all-reduce.4
  818.4 197.0 all-reduce.4
  1036.3 96.4 all-reduce.2
where the time goes:
time: 1150 us; the launch traced here: 1140 us
  waiting for transfers between devices  910 us (79%)
  other arithmetic  115 us (10%)
  matrix products  72.7 us (6%)
  local copies, waits for them, and re-layouts  32 us (3%)
  between operations  14.1 us (1%)
    psum x4, waiting for transfers between devices, from_root(): return lax.psum(kept, axis)  657 us
    all_gather x1, waiting for transfers between devices, local(): full_rows = lax.all_gather(lower, 'ga', axis=1, tiled=True)  155 us
    psum x1, waiting for transfers between devices, local(): lax.psum(local_intersection, 'ga') / (width * lax.axis_size('ga'))  96.6 us
    another operation x3, other arithmetic, finish(): return jax.scipy.linalg.solve_triangular(own_tile, rhs, lower=True)  83.3 us
    dot_general x4, matrix products, section(): jnp.dot(tile, arrived, precision=lax.Precision.HIGHEST, preferred_element...  41.1 us
    another operation x27, local copies, waits for them, and re-layouts  27.2 us
  transfers between devices with their start and end apart: 6, of which 6 were waited for; matrix products, arithmetic and copies ran while one was open for 0% of the time, Pallas kernels for 0%

commit v1 on v0

v1 whole, which is shorter than its diff:
```python
import jax
import jax.numpy as jnp
from jax import lax
from jax.sharding import PartitionSpec as P

BASE = 128
PIECES = 2


def mm(a, b, precision):
    return jnp.matmul(a, b, precision=precision, preferred_element_type=jnp.float32)


def tri_inverse(tile):
    n = tile.shape[0]
    base = min(BASE, n)
    best = lax.Precision.HIGHEST
    blocks = jnp.stack([tile[i : i + base, i : i + base] for i in range(0, n, base)])
    row = lax.broadcasted_iota(jnp.int32, (base, base), 0)
    col = lax.broadcasted_iota(jnp.int32, (base, base), 1)
    inverse = jnp.where(row == col, 1.0 / jnp.where(row == col, blocks, 1.0), 0.0)
    size = 1
    while size < base:
        off = (row // (2 * size) == col // (2 * size)) & (row // size > col // size)
        below = jnp.where(off, blocks, 0.0)
        inverse = inverse - mm(inverse, mm(below, inverse, best), best)
        size *= 2
    while size < n:
        below = jnp.stack(
            [tile[i + size : i + 2 * size, i : i + size] for i in range(0, n, 2 * size)]
        )
        first, second = inverse[0::2], inverse[1::2]
        corner = -mm(second, mm(below, first, best), best)
        top = jnp.concatenate([first, jnp.zeros_like(first)], axis=2)
        bottom = jnp.concatenate([corner, second], axis=2)
        inverse = jnp.concatenate([top, bottom], axis=1)
        size *= 2
    return inverse[0]


def local(psi, lower):
    high = lax.Precision.HIGH
    myblock = lax.axis_index("band")
    sections = lax.axis_size("band")
    nrows, width = psi.shape
    full_rows = lax.all_gather(lower, "ga", axis=1, tiled=True)
    own_tile = lax.dynamic_slice_in_dim(full_rows, myblock * nrows, nrows, 1)
    inverse = tri_inverse(own_tile)
    span = width // PIECES
    rest = [psi[:, i * span : (i + 1) * span] for i in range(PIECES)]
    for s in range(sections - 1):
        tile = full_rows[:, s * nrows : (s + 1) * nrows]
        for i in range(PIECES):
            ready = mm(inverse, rest[i], high)
            arrived = lax.ppermute(ready, "band", [(s, s + 1)])
            for t in range(s + 2, sections):
                arrived = arrived + lax.ppermute(ready, "band", [(s, t)])
            rest[i] = rest[i] - mm(tile, arrived, high)
    solved = jnp.concatenate([mm(inverse, rest[i], high) for i in range(PIECES)], axis=1)
    mine = lax.dot_general(
        solved, solved, (((1,), (1,)), ((), ())), precision=high, preferred_element_type=jnp.float32
    )
    intersection = lax.psum(mine, "ga") / (width * lax.axis_size("ga"))
    return (solved, intersection)


def solution(mesh):
    return jax.shard_map(
        local,
        mesh=mesh,
        in_specs=(P("band", "ga"), P("band", "ga")),
        out_specs=(P("band", "ga"), P("band", None)),
        check_vma=False,
    )
```

time: 1150 us -> 485 us (0.42)
  waiting for transfers between devices: 910 us -> 352 us
  other arithmetic: 115 us -> 7.41 us
  starting transfers between devices: 0.05 us -> 20.3 us
  local copies, waits for them, and re-layouts: 32 us -> 12.7 us
    psum x5 -> x1, waiting for transfers between devices: 754 us -> 131 us  [local(): intersection = lax.psum(mine, 'ga') / (width * lax.axis_size('ga'))]
    another operation x3 -> x0, other arithmetic: 83.3 us -> none  [finish(): return jax.scipy.linalg.solve_triangular(own_tile, rhs, lower=True)]
    ppermute x0 -> x12, waiting for transfers between devices: none -> 64.6 us  [the longest x6 40.7 us: local(): arrived = arrived + lax.ppermute(ready, 'band', [(s, t)])]
    another operation x28 -> x3, local copies, waits for them, and re-layouts: 27.2 us -> 2.9 us  [the longest x2 2.05 us: tri_inverse(): jnp.stack([tile[i + size:i + 2 * size, i:i + size] for i in range(0, n, 2...]
    another operation x15 -> x0, matrix products: 21.2 us -> none  [finish(): return jax.scipy.linalg.solve_triangular(own_tile, rhs, lower=True)]
    ppermute x0 -> x12, starting transfers between devices: none -> 20.2 us  [the longest x6 11.1 us: local(): arrived = arrived + lax.ppermute(ready, 'band', [(s, t)])]
    select_n x4 -> x0, other arithmetic: 19.1 us -> none  [section(): new_results = [jnp.where(myblock == section_idx, ready, results[0])]]
    dot_general x5 -> x35, matrix products: 51.5 us -> 68.4 us  [the longest x34 63.1 us: mm(): jnp.matmul(a, b, precision=precision, preferred_element_type=jnp.float32)]
  transfers between devices with their start and end apart: 6 -> 14, of which waited for: 6 -> 7; matrix products, arithmetic and copies ran while one was open for 0% -> 9% of each run, Pallas kernels for 0% -> 0%
where the time goes in v1:
time: 485 us; the launch traced here: 476 us
  waiting for transfers between devices  352 us (73%)
  matrix products  68.4 us (14%)
  starting transfers between devices  20.3 us (4%)
  between operations  15.2 us (3%)
  local copies, waits for them, and re-layouts  12.7 us (3%)
  other arithmetic  7.41 us (2%)
    all_gather x1, waiting for transfers between devices, local(): full_rows = lax.all_gather(lower, 'ga', axis=1, tiled=True)  155 us
    psum x1, waiting for transfers between devices, local(): intersection = lax.psum(mine, 'ga') / (width * lax.axis_size('ga'))  131 us
    dot_general x34, matrix products, mm(): jnp.matmul(a, b, precision=precision, preferred_element_type=jnp.float32)  63.1 us
    ppermute x6, waiting for transfers between devices, local(): arrived = arrived + lax.ppermute(ready, 'band', [(s, t)])  40.7 us
    ppermute x6, waiting for transfers between devices, local(): arrived = lax.ppermute(ready, 'band', [(s, s + 1)])  23.9 us
    ppermute x6, starting transfers between devices, local(): arrived = arrived + lax.ppermute(ready, 'band', [(s, t)])  11.1 us
  transfers between devices with their start and end apart: 14, of which 7 were waited for; matrix products, arithmetic and copies ran while one was open for 9% of the time, Pallas kernels for 0%

profile of v1, /device:TPU:0, one launch (start us, length us, event | category | flops | bytes accessed | tf_op | source)
XLA Modules:
  0.0 475.6 jit_solution(3111644999195573974)
XLA Ops:
  8.7 154.8 %all-gather.2.cloned.1.call-done = f32[1024,4096]{1,0:T(8,128)} async-done(((f32[1024,512]{1,0:T(8,128)}), f32[1024,4096]{1,0:T(8,128)}) %all-gather.2.cloned.1.call-update) | async-done | bytes 16777232 | tf_op jit(solution)/shard_map/all_gather | solution.py:46
  185.5 3.9 fusion.50
  189.4 1.9 fusion.49
  191.2 2.8 fusion.141
  194.1 3.4 collective-permute-start
  197.5 2.3 collective-permute-start.1
  199.8 2.3 collective-permute-start.2
  202.1 2.8 fusion.139
  204.9 2.2 collective-permute-start.6
  207.1 2.3 collective-permute-start.7
  209.4 11.9 %collective-permute-done = f32[1024,256]{1,0:T(8,128)S(1)} collective-permute-done((f32[1024,256]{1,0:T(8,128)}, f32[1024,256]{1,0:T(8,128)S(1)}, u32[]{:S(2)}, u32[]{:S(2)}) %collective-permute-start) | collective-permute-done | bytes 1048608 | tf_op jit(solution)/shard_map/ppermute | solution.py:55
  221.3 2.7 collective-permute-start.8
  224.8 18.9 %collective-permute-done.2 = f32[1024,256]{1,0:T(8,128)} collective-permute-done((f32[1024,256]{1,0:T(8,128)}, f32[1024,256]{1,0:T(8,128)}, u32[]{:S(2)}, u32[]{:S(2)}) %collective-permute-start.2) | collective-permute-done | bytes 1048608 | tf_op jit(solution)/shard_map/ppermute | solution.py:57
  243.7 6.8 %fusion.16 = f32[1024,256]{0,1:T(8,128)S(1)} fusion(f32[1024,256]{0,1:T(8,128)S(1)} %copy.13, f32[1024,4096]{1,0:T(8,128)} %all-gather.2.cloned.1.call-done, f32[1024,256]{1,0:T(8,128)} %collective-permute-done.2, f32[1024,256]{1,0:T(8,128)} %copy-done.4, f32[1024,256]{1,0:T(8,128)} %collective-permute-done.1), kind=kOutput, calls=%fused_computation.20 | convolution fusion | flops 1611399168 | bytes 9437184 | tf_op jit(solution)/shard_map/dot_general | solution.py:11
  250.6 1.9 fusion.155
  254.2 12.0 %collective-permute-done.6 = f32[1024,256]{1,0:T(8,128)} collective-permute-done((f32[1024,256]{1,0:T(8,128)}, f32[1024,256]{1,0:T(8,128)}, u32[]{:S(2)}, u32[]{:S(2)}) %collective-permute-start.6) | collective-permute-done | bytes 1048608 | tf_op jit(solution)/shard_map/ppermute | solution.py:55
  266.9 21.2 %collective-permute-done.8 = f32[1024,256]{1,0:T(8,128)} collective-permute-done((f32[1024,256]{1,0:T(8,128)}, f32[1024,256]{1,0:T(8,128)}, u32[]{:S(2)}, u32[]{:S(2)}) %collective-permute-start.8) | collective-permute-done | bytes 1048608 | tf_op jit(solution)/shard_map/ppermute | solution.py:57
  288.0 6.7 %fusion.22 = f32[1024,256]{0,1:T(8,128)S(1)} fusion(f32[1024,256]{0,1:T(8,128)S(1)} %copy.14, f32[1024,4096]{1,0:T(8,128)} %all-gather.2.cloned.1.call-done, f32[1024,256]{1,0:T(8,128)} %collective-permute-done.8, f32[1024,256]{1,0:T(8,128)} %collective-permute-done.6, f32[1024,256]{1,0:T(8,128)} %collective-permute-done.7), kind=kOutput, calls=%fused_computation.22 | convolution fusion | flops 1611399168 | bytes 9437184 | tf_op jit(solution)/shard_map/dot_general | solution.py:11
  294.7 1.9 fusion.148
  298.3 3.7 fusion.28
  301.9 1.9 fusion.153
  304.6 3.7 fusion.34
  308.2 1.9 fusion.146
  311.1 3.7 fusion.40
  314.7 1.9 fusion.151
  316.6 3.7 fusion.46
  320.3 1.9 fusion.144
  323.2 5.3 %fusion.143 = f32[1024,1024]{1,0:T(8,128)} fusion(f32[1024,256]{0,1:T(8,128)S(1)} %fusion.144, f32[1024,256]{0,1:T(8,128)S(1)} %fusion.151), kind=kOutput, calls=%fused_computation.196 | convolution fusion | flops 3221749760 | bytes 6291456 | tf_op jit(solution)/shard_map/dot_general | solution.py:60
  328.6 1.4 pad_maximum_fusion
  330.0 1.8 copy.9
  331.8 131.5 %all-reduce.5.cloned.1.call-done = f32[1024,1024]{1,0:T(8,128)} async-done(((f32[1024,1024]{1,0:T(8,128)}), f32[1024,1024]{1,0:T(8,128)}) %all-reduce.5.cloned.1.call-update) | async-done | bytes 4194320 | tf_op jit(solution)/shard_map/psum | solution.py:63
  463.3 5.0 %broadcast_multiply_fusion = f32[1024,1024]{1,0:T(8,128)} fusion(f32[1024,1024]{1,0:T(8,128)} %all-reduce.5.cloned.1.call-done), kind=kLoop, calls=%fused_computation.18 | loop fusion | flops 1048576 | bytes 8388608 | tf_op jit(solution)/shard_map/div | solution.py:63
  (95 shorter events, 30.8 us)
Async XLA Ops:
  7.2 156.3 %all-gather.2.cloned.1.call-start = ((), (), s32[]{:S(2)}) async-start(), calls=%async_computation | async-start | bytes 18874368 | tf_op jit(solution)/shard_map/all_gather | solution.py:46
  7.9 455.4 %all-reduce.5.cloned.1.call-start = ((), (), s32[]{:S(2)}) async-start(), calls=%async_computation.1 | async-start | bytes 8388608 | tf_op jit(solution)/shard_map/psum | solution.py:63
  185.5 16.6 %copy-start.5 = (f32[1,512,512]{2,1,0:T(8,128)}, f32[1,512,512]{2,1,0:T(8,128)S(1)}, u32[]{:S(2)}) copy-start(f32[1,512,512]{2,1,0:T(8,128)S(1)} %get-tuple-element.12) | copy-start | bytes 3145732
  185.5 16.6 %copy-start.7 = (f32[1,512,512]{2,1,0:T(8,128)}, f32[1,512,512]{2,1,0:T(8,128)S(1)}, u32[]{:S(2)}) copy-start(f32[1,512,512]{2,1,0:T(8,128)S(1)} %get-tuple-element.13) | copy-start | bytes 3145732
  185.5 5.7 %copy-start.1 = (f32[1024,512]{1,0:T(8,128)S(1)}, f32[1024,512]{1,0:T(8,128)}, u32[]{:S(2)}) copy-start(f32[1024,512]{1,0:T(8,128)} %param.2) | copy-start | bytes 6291460
  191.2 10.9 %copy-start.2 = (f32[1,512,512]{2,1,0:T(8,128)}, f32[1,512,512]{2,1,0:T(8,128)S(1)}, u32[]{:S(2)}) copy-start(f32[1,512,512]{2,1,0:T(8,128)S(1)} %fusion.49) | copy-start | bytes 3145732
  194.1 27.2 %collective-permute-start = (f32[1024,256]{1,0:T(8,128)}, f32[1024,256]{1,0:T(8,128)S(1)}, u32[]{:S(2)}, u32[]{:S(2)}) collective-permute-start(f32[1024,256]{1,0:T(8,128)} %fusion.141), channel_id=1, source_target_pairs={{0,8},{1,9},{2,10},{3,11},{4,12},{5,13},{6,14},{7,15}} | collective-permute-start | bytes 3145736 | tf_op jit(solution)/shard_map/ppermute | solution.py:55
  197.5 27.3 %collective-permute-start.1 = (f32[1024,256]{1,0:T(8,128)}, f32[1024,256]{1,0:T(8,128)}, u32[]{:S(2)}, u32[]{:S(2)}) collective-permute-start(f32[1024,256]{1,0:T(8,128)} %fusion.141), channel_id=1, source_target_pairs={{0,16},{1,17},{2,18},{3,19},{4,20},{5,21},{6,22},{7,23}} | collective-permute-start | bytes 3145736 | tf_op jit(solution)/shard_map/ppermute | solution.py:57
  199.8 43.9 %collective-permute-start.2 = (f32[1024,256]{1,0:T(8,128)}, f32[1024,256]{1,0:T(8,128)}, u32[]{:S(2)}, u32[]{:S(2)}) collective-permute-start(f32[1024,256]{1,0:T(8,128)} %fusion.141), channel_id=1, source_target_pairs={{0,24},{1,25},{2,26},{3,27},{4,28},{5,29},{6,30},{7,31}} | collective-permute-start | bytes 3145736 | tf_op jit(solution)/shard_map/ppermute | solution.py:57
  204.9 61.3 %collective-permute-start.6 = (f32[1024,256]{1,0:T(8,128)}, f32[1024,256]{1,0:T(8,128)}, u32[]{:S(2)}, u32[]{:S(2)}) collective-permute-start(f32[1024,256]{1,0:T(8,128)} %fusion.139), channel_id=1, source_target_pairs={{0,8},{1,9},{2,10},{3,11},{4,12},{5,13},{6,14},{7,15}} | collective-permute-start | bytes 3145736 | tf_op jit(solution)/shard_map/ppermute | solution.py:55
  207.1 59.7 %collective-permute-start.7 = (f32[1024,256]{1,0:T(8,128)}, f32[1024,256]{1,0:T(8,128)}, u32[]{:S(2)}, u32[]{:S(2)}) collective-permute-start(f32[1024,256]{1,0:T(8,128)} %fusion.139), channel_id=1, source_target_pairs={{0,16},{1,17},{2,18},{3,19},{4,20},{5,21},{6,22},{7,23}} | collective-permute-start | bytes 3145736 | tf_op jit(solution)/shard_map/ppermute | solution.py:57
  221.3 2.8 copy-start.4
  221.3 66.7 %collective-permute-start.8 = (f32[1024,256]{1,0:T(8,128)}, f32[1024,256]{1,0:T(8,128)}, u32[]{:S(2)}, u32[]{:S(2)}) collective-permute-start(f32[1024,256]{1,0:T(8,128)} %fusion.139), channel_id=1, source_target_pairs={{0,24},{1,25},{2,26},{3,27},{4,28},{5,29},{6,30},{7,31}} | collective-permute-start | bytes 3145736 | tf_op jit(solution)/shard_map/ppermute | solution.py:57
  224.8 25.8 %copy-start.3 = (f32[1,512,512]{2,1,0:T(8,128)S(1)}, f32[1,512,512]{2,1,0:T(8,128)}, u32[]{:S(2)}) copy-start(f32[1,512,512]{2,1,0:T(8,128)} %copy-done.2) | copy-start | bytes 3145732
  224.8 25.8 %copy-start.6 = (f32[1,512,512]{2,1,0:T(8,128)S(1)}, f32[1,512,512]{2,1,0:T(8,128)}, u32[]{:S(2)}) copy-start(f32[1,512,512]{2,1,0:T(8,128)} %copy-done.5) | copy-start | bytes 3145732
  224.8 25.8 %copy-start.8 = (f32[1,512,512]{2,1,0:T(8,128)S(1)}, f32[1,512,512]{2,1,0:T(8,128)}, u32[]{:S(2)}) copy-start(f32[1,512,512]{2,1,0:T(8,128)} %copy-done.7) | copy-start | bytes 3145732
  243.7 54.5 %slice-start = ((s8[16777216]{0:T(1024)(128)(4,1)}), s8[4194304]{0:T(1024)(128)(4,1)S(1)}, s32[]{:S(2)}) async-start(s8[16777216]{0:T(1024)(128)(4,1)} %bitcast.116), calls=%async_computation.2 | async-start | bytes 8388608
  250.6 47.7 %slice-start.1 = ((s8[16777216]{0:T(1024)(128)(4,1)}), s8[4194304]{0:T(1024)(128)(4,1)S(1)}, s32[]{:S(2)}) async-start(s8[16777216]{0:T(1024)(128)(4,1)} %bitcast.116), calls=%async_computation.3 | async-start | bytes 8388608
  252.5 45.8 %slice-start.2 = ((s8[16777216]{0:T(1024)(128)(4,1)}), s8[4194304]{0:T(1024)(128)(4,1)S(1)}, s32[]{:S(2)}) async-start(s8[16777216]{0:T(1024)(128)(4,1)} %bitcast.116), calls=%async_computation.4 | async-start | bytes 8388608
  252.5 45.7 %collective-permute-start.3 = (f32[1024,256]{1,0:T(8,128)S(1)}, f32[1024,256]{1,0:T(8,128)S(1)}, u32[]{:S(2)}, u32[]{:S(2)}) collective-permute-start(f32[1024,256]{1,0:T(8,128)S(1)} %fusion.155), channel_id=1, source_target_pairs={{8,16},{9,17},{10,18},{11,19},{12,20},{13,21},{14,22},{15,23}} | collective-permute-start | bytes 3145736 | tf_op jit(solution)/shard_map/ppermute | solution.py:55
  253.3 44.9 %collective-permute-start.4 = (f32[1024,256]{1,0:T(8,128)S(1)}, f32[1024,256]{1,0:T(8,128)S(1)}, u32[]{:S(2)}, u32[]{:S(2)}) collective-permute-start(f32[1024,256]{1,0:T(8,128)S(1)} %fusion.155), channel_id=1, source_target_pairs={{8,24},{9,25},{10,26},{11,27},{12,28},{13,29},{14,30},{15,31}} | collective-permute-start | bytes 3145736 | tf_op jit(solution)/shard_map/ppermute | solution.py:57
  294.7 3.6 slice-start.3
  296.6 8.0 %collective-permute-start.10 = (f32[1024,256]{1,0:T(8,128)S(1)}, f32[1024,256]{1,0:T(8,128)S(1)}, u32[]{:S(2)}, u32[]{:S(2)}) collective-permute-start(f32[1024,256]{1,0:T(8,128)S(1)} %fusion.148), channel_id=1, source_target_pairs={{8,24},{9,25},{10,26},{11,27},{12,28},{13,29},{14,30},{15,31}} | collective-permute-start | bytes 3145736 | tf_op jit(solution)/shard_map/ppermute | solution.py:57
  297.3 7.3 %collective-permute-start.9 = (f32[1024,256]{1,0:T(8,128)S(1)}, f32[1024,256]{1,0:T(8,128)S(1)}, u32[]{:S(2)}, u32[]{:S(2)}) collective-permute-start(f32[1024,256]{1,0:T(8,128)S(1)} %fusion.148), channel_id=1, source_target_pairs={{8,16},{9,17},{10,18},{11,19},{12,20},{13,21},{14,22},{15,23}} | collective-permute-start | bytes 3145736 | tf_op jit(solution)/shard_map/ppermute | solution.py:55
  303.8 7.2 %collective-permute-start.5 = (f32[1024,256]{1,0:T(8,128)S(1)}, f32[1024,256]{1,0:T(8,128)S(1)}, u32[]{:S(2)}, u32[]{:S(2)}) collective-permute-start(f32[1024,256]{1,0:T(8,128)S(1)} %fusion.153), channel_id=1, source_target_pairs={{16,24},{17,25},{18,26},{19,27},{20,28},{21,29},{22,30},{23,31}} | collective-permute-start | bytes 3145736 | tf_op jit(solution)/shard_map/ppermute | solution.py:55
  310.1 6.5 %collective-permute-start.11 = (f32[1024,256]{1,0:T(8,128)S(1)}, f32[1024,256]{1,0:T(8,128)S(1)}, u32[]{:S(2)}, u32[]{:S(2)}) collective-permute-start(f32[1024,256]{1,0:T(8,128)S(1)} %fusion.146), channel_id=1, source_target_pairs={{16,24},{17,25},{18,26},{19,27},{20,28},{21,29},{22,30},{23,31}} | collective-permute-start | bytes 3145736 | tf_op jit(solution)/shard_map/ppermute | solution.py:55
  322.2 1.0 copy-start
Sparse Core Ops, SparseCore 0:
  9.6 153.7 all-gather.1
  328.7 134.5 all-reduce.4
